TPU v7x, 32 devices: a whole 2x2x4 slice. The times are simulated.
32 devices in a mesh: rel: 4 (over y, x), node: 4 (over z), feat: 2 (over core).
Axes of the slice: x: 2, y: 2, z: 4, core: 2. Of those that a mesh axis runs over, the one named last changes fastest.
Arguments:
- features: float32 [3072, 768], P('node', 'feat'), may hold values from -6 to 6
- tile_values: float32 [4, 12, 12, 256, 256], P('rel', 'node'), may hold values from -0.4375 to 0.4375
- tile_cols: int32 [4, 12, 12], P('rel', 'node'), may hold values from 0 to 11, as said below
- tile_count: int32 [4, 12], P('rel', 'node'), may hold values from 1 to 12, as said below
- degree: int32 [4, 3072], P('rel', 'node'), may hold values from 1 to 16
- proj_weight: float32 [4, 768, 512], P('rel', 'feat'), may hold values from -0.21875 to 0.21875
- proj_bias: float32 [4, 512], P('rel', 'feat'), may hold values from -3 to 3
Outputs:
- metapath_out: float32 [4, 3072, 512], P(None, ('node', 'rel'), 'feat')
Inputs may be any that keep to these rules, and one draw needn't show every extreme that they name: `tile_cols`: within one row of tiles the 12 column tiles are distinct; slots at or past the count hold valid tile numbers that are not used. `tile_count`: in every relation some row of tiles has exactly 12 live slots.
All inputs are finite; a program needn't handle non-finite values.
Results may differ from a plain program's by a relative error of at most 0.0001.
Values sent between devices are 32-bit elements; how exact they have to be, the bound alone decides.
A program may use at most 128 MiB of HBM per device.

v0:
```python
import jax
import jax.numpy as jnp
from jax import lax
from jax.sharding import PartitionSpec as P


def spread(gathered, masked, col_tiles):
    columns = gathered.shape[1]
    tile_rows = gathered.reshape(-1, masked.shape[2], columns)
    sources = jnp.take(tile_rows, col_tiles, axis=0)
    summed = jnp.einsum(
        "tkab,tkbw->taw",
        masked,
        sources,
        precision=lax.Precision.HIGH,
        preferred_element_type=jnp.float32,
    )
    return summed.reshape(-1, columns)


def on_device(features, tile_values, tile_cols, tile_count, degree, proj_weight, proj_bias):
    row_scale = lax.rsqrt(degree[0].astype(jnp.float32))[:, None]
    counts = tile_count[0]
    live_mask = (jnp.arange(tile_values.shape[2])[None, :] < counts[:, None]).astype(jnp.float32)
    masked = tile_values[0] * live_mask[:, :, None, None]
    col_tiles = tile_cols[0]
    partial_sum = jnp.dot(
        features, proj_weight[0], precision=lax.Precision.HIGH, preferred_element_type=jnp.float32
    )
    current = lax.psum_scatter(partial_sum, "feat", scatter_dimension=1, tiled=True)
    for hop_index in range(2):
        gathered = lax.all_gather(row_scale * current, "node", axis=0, tiled=True)
        current = row_scale * spread(gathered, masked, col_tiles)
    result = current + proj_bias[0][None, :]
    return lax.all_to_all(result[None], "rel", split_axis=1, concat_axis=0, tiled=True)


def solution(mesh):
    return jax.shard_map(
        on_device,
        mesh=mesh,
        in_specs=(
            P("node", "feat"),
            P("rel", "node", None, None, None),
            P("rel", "node", None),
            P("rel", "node"),
            P("rel", "node"),
            P("rel", "feat", None),
            P("rel", "feat"),
        ),
        out_specs=P(None, ("node", "rel"), "feat"),
        check_vma=False,
    )
```

profile of v0, /device:TPU:0, one launch (start us, length us, event | category | flops | bytes accessed | tf_op | source)
XLA Modules:
  0.0 216.2 jit_solution(5188851948771330307)
XLA Ops:
  6.5 0.0 copy-start
  6.5 0.0 reduce-scatter.2.cloned.1.call-start
  6.5 1.3 copy-done
  7.8 3.7 %fusion.11 = f32[768,512]{1,0:T(8,128)} fusion(f32[768,384]{1,0:T(8,128)S(1)} %copy-done, f32[1,384,512]{2,1,0:T(8,128)} %param.14), kind=kOutput, calls=%fused_computation.15 | convolution fusion | flops 905969664 | bytes 3538944 | tf_op jit(solution)/shard_map/dot_general | solution.py:27
  11.5 0.0 reduce-scatter.2.cloned.1.call-update
  11.5 0.0 all-gather.3.cloned.1.call-start
  11.6 0.7 rsqrt_reduce_fusion
  12.3 11.1 %reduce-scatter.2.cloned.1.call-done = f32[768,256]{1,0:T(8,128)} async-done(((f32[768,512]{1,0:T(8,128)}), f32[768,256]{1,0:T(8,128)}) %reduce-scatter.2.cloned.1.call-update) | async-done | bytes 786448 | tf_op jit(solution)/shard_map/reduce_scatter | solution.py:30
  23.4 2.2 %broadcast_multiply_fusion = f32[768,256]{1,0:T(8,128)} fusion(f32[768,256]{1,0:T(8,128)} %reduce-scatter.2.cloned.1.call-done, f32[768]{0:T(1024)S(1)} %rsqrt_reduce_fusion), kind=kLoop, calls=%fused_computation.18 | loop fusion | flops 196608 | bytes 1575936 | tf_op jit(solution)/shard_map/mul | solution.py:32
  25.6 0.0 all-gather.3.cloned.1.call-update
  25.6 0.0 all-gather.5.cloned.1.call-start
  25.7 0.7 compare_select_fusion
  26.4 0.1 reshape.133
  26.5 0.8 fusion.13
  27.2 63.3 %all-gather.3.cloned.1.call-done = f32[3072,256]{1,0:T(8,128)} async-done(((f32[768,256]{1,0:T(8,128)}), f32[3072,256]{1,0:T(8,128)}) %all-gather.3.cloned.1.call-update) | async-done | bytes 3145744 | tf_op jit(solution)/shard_map/all_gather | solution.py:32
  90.5 8.6 %gather_fusion = f32[36,256,256]{2,1,0:T(8,128)} fusion(f32[12,256,256]{2,1,0:T(8,128)} %bitcast.32, s32[1024]{0:T(1024)S(1)} %pad_clamp_fusion), kind=kCustom, calls=%fused_computation.clone | custom fusion | bytes 18874512 | tf_op jit(solution)/shard_map/jit(_take)/gather | solution.py:10
  99.1 11.0 %fusion.2 = f32[3,256,256,1]{2,1,3,0:T(8,128)S(1)} fusion(f32[3,12,256,256]{3,2,1,0:T(8,128)} %bitcast.31, f32[1,3,12,256,256]{4,3,2,1,0:T(8,128)} %param.10, f32[3,12]{1,0:T(4,128)S(1)} %get-tuple-element.6, pred[3,12]{1,0:T(4,128)(4,1)S(1)} %get-tuple-element.7), kind=kOutput, calls=%fused_computation.5 | convolution fusion | flops 3628597248 | bytes 19660980 | tf_op jit(solution)/shard_map/tkab,tkbw->taw/dot_general | solution.py:11
  110.1 1.1 fusion.10
  111.1 0.0 all-gather.5.cloned.1.call-update
  111.1 62.3 %all-gather.5.cloned.1.call-done = f32[3072,256]{1,0:T(8,128)} async-done(((f32[768,256]{1,0:T(8,128)}), f32[3072,256]{1,0:T(8,128)}) %all-gather.5.cloned.1.call-update) | async-done | bytes 3145744 | tf_op jit(solution)/shard_map/all_gather | solution.py:32
  173.5 8.6 %gather_fusion.1 = f32[36,256,256]{2,1,0:T(8,128)} fusion(f32[12,256,256]{2,1,0:T(8,128)} %bitcast.33, s32[1024]{0:T(1024)S(1)} %pad_clamp_fusion), kind=kCustom, calls=%fused_computation.1.clone | custom fusion | bytes 18874512 | tf_op jit(solution)/shard_map/jit(_take)/gather | solution.py:10
  182.0 0.0 copy-start.1
  182.0 11.0 %fusion = f32[3,256,256,1]{2,1,3,0:T(8,128)S(1)} fusion(f32[3,12,256,256]{3,2,1,0:T(8,128)} %bitcast.30, f32[1,3,12,256,256]{4,3,2,1,0:T(8,128)} %param.10, f32[3,12]{1,0:T(4,128)S(1)} %get-tuple-element.6, pred[3,12]{1,0:T(4,128)(4,1)S(1)} %get-tuple-element.7), kind=kOutput, calls=%fused_computation.3 | convolution fusion | flops 3628597248 | bytes 19660980 | tf_op jit(solution)/shard_map/tkab,tkbw->taw/dot_general | solution.py:11
  193.0 0.0 copy-done.1
  193.0 0.2 multiply_add_fusion
  193.2 0.8 copy.9
  194.0 14.7 %all_to_all.12 = f32[1,768,256]{2,0,1:T(1,128)S(1)} all-to-all(f32[1,768,256]{2,0,1:T(1,128)S(1)} %copy.9), channel_id=1, replica_groups=mesh['rel'=4,'node'=4,'feat'=2] {'rel'}, dimensions={1} | all-to-all | bytes 1572864 | tf_op jit(solution)/shard_map/all_to_all | solution.py:35
  208.8 0.9 copy.13
  (1 shorter events, 0.0 us)
Async XLA Ops:
  6.5 1.3 copy-start
  6.5 16.9 %reduce-scatter.2.cloned.1.call-start = ((), (), s32[]{:S(2)}) async-start(), calls=%async_computation.2 | async-start | bytes 2359296 | tf_op jit(solution)/shard_map/reduce_scatter | solution.py:30
  11.5 79.0 %all-gather.3.cloned.1.call-start = ((), (), s32[]{:S(2)}) async-start(), calls=%async_computation.3 | async-start | bytes 3932160 | tf_op jit(solution)/shard_map/all_gather | solution.py:32
  25.6 147.8 %all-gather.5.cloned.1.call-start = ((), (), s32[]{:S(2)}) async-start(), calls=%async_computation.4 | async-start | bytes 3932160 | tf_op jit(solution)/shard_map/all_gather | solution.py:32
  182.0 11.0 %copy-start.1 = (f32[1,256]{1,0:T(1,128)S(1)}, f32[1,256]{1,0:T(1,128)}, u32[]{:S(2)}) copy-start(f32[1,256]{1,0:T(1,128)} %param.15) | copy-start | bytes 3076
Sparse Core Ops, SparseCore 0:
  11.6 11.7 reduce-scatter.1
  25.8 64.7 all-gather.2
  111.3 62.1 all-gather.4
where the time goes:
time: 217 us; the launch traced here: 216 us
  waiting for transfers between devices  137 us (63%)
  matrix products  25.6 us (12%)
  local copies, waits for them, and re-layouts  20.3 us (9%)
  blocking collectives  14.7 us (7%)
  between operations  13.2 us (6%)
  other arithmetic  5.56 us (3%)
    all_gather x2, waiting for transfers between devices, on_device(): gathered = lax.all_gather(row_scale * current, 'node', axis=0, tiled=True)  126 us
    dot_general x2, matrix products, spread(): jnp.einsum('tkab,tkbw->taw', masked, sources, precision=lax.Precision.HIG...  21.9 us
    gather x2, local copies, waits for them, and re-layouts, spread(): sources = jnp.take(tile_rows, col_tiles, axis=0)  17.2 us
    all_to_all x1, blocking collectives, on_device(): lax.all_to_all(result[None], 'rel', split_axis=1, concat_axis=0, tiled=True)  14.7 us
    reduce_scatter x1, waiting for transfers between devices, on_device(): lax.psum_scatter(partial_sum, 'feat', scatter_dimension=1, tiled=True)  11.1 us
  transfers between devices with their start and end apart: 3, of which 3 were waited for; matrix products, arithmetic and copies ran while one was open for 1% of the time, Pallas kernels for 0%

commit v1 on v0

--- a/solution.py
+++ b/solution.py
@@ -2,6 +2,13 @@
 import jax.numpy as jnp
 from jax import lax
 from jax.sharding import PartitionSpec as P
+
+
+def swap_blocks(x, axis, split, join):
+    devices = lax.axis_size(axis)
+    blocks = jnp.stack(jnp.split(x, devices, axis=split), axis=0)
+    blocks = lax.all_to_all(blocks, axis, split_axis=0, concat_axis=0)
+    return jnp.concatenate(blocks, axis=join)
 
 
 def spread(gathered, masked, col_tiles):
@@ -32,7 +39,7 @@
         gathered = lax.all_gather(row_scale * current, "node", axis=0, tiled=True)
         current = row_scale * spread(gathered, masked, col_tiles)
     result = current + proj_bias[0][None, :]
-    return lax.all_to_all(result[None], "rel", split_axis=1, concat_axis=0, tiled=True)
+    return swap_blocks(result[None], "rel", 1, 0)
 
 
 def solution(mesh):

time: 217 us -> 216 us (level)
  no operation moved by 1% of the time
where the time goes in v1:
time: 216 us; the launch traced here: 215 us
  waiting for transfers between devices  137 us (63%)
  matrix products  25.6 us (12%)
  local copies, waits for them, and re-layouts  19.4 us (9%)
  blocking collectives  14.7 us (7%)
  between operations  13.2 us (6%)
  other arithmetic  5.62 us (3%)
    all_gather x2, waiting for transfers between devices, on_device(): gathered = lax.all_gather(row_scale * current, 'node', axis=0, tiled=True)  126 us
    dot_general x2, matrix products, spread(): jnp.einsum('tkab,tkbw->taw', masked, sources, precision=lax.Precision.HIG...  21.9 us
    gather x2, local copies, waits for them, and re-layouts, spread(): sources = jnp.take(tile_rows, col_tiles, axis=0)  17.2 us
    all_to_all x1, blocking collectives, swap_blocks(): blocks = lax.all_to_all(blocks, axis, split_axis=0, concat_axis=0)  14.7 us
    reduce_scatter x1, waiting for transfers between devices, on_device(): lax.psum_scatter(partial_sum, 'feat', scatter_dimension=1, tiled=True)  11.1 us
  transfers between devices with their start and end apart: 3, of which 3 were waited for; matrix products, arithmetic and copies ran while one was open for 1% of the time, Pallas kernels for 0%

profile of v1, /device:TPU:0, one launch (start us, length us, event | category | flops | bytes accessed | tf_op | source)
XLA Modules:
  0.0 215.5 jit_solution(13550042795787411703)
XLA Ops:
  6.5 0.0 copy-start
  6.5 0.0 reduce-scatter.2.cloned.1.call-start
  6.5 1.3 copy-done
  7.8 3.7 %fusion.11 = f32[768,512]{1,0:T(8,128)} fusion(f32[768,384]{1,0:T(8,128)S(1)} %copy-done, f32[1,384,512]{2,1,0:T(8,128)} %param.14), kind=kOutput, calls=%fused_computation.16 | convolution fusion | flops 905969664 | bytes 3538944 | tf_op jit(solution)/shard_map/dot_general | solution.py:34
  11.5 0.0 reduce-scatter.2.cloned.1.call-update
  11.5 0.0 all-gather.3.cloned.1.call-start
  11.6 0.7 rsqrt_reduce_fusion
  12.3 11.1 %reduce-scatter.2.cloned.1.call-done = f32[768,256]{1,0:T(8,128)} async-done(((f32[768,512]{1,0:T(8,128)}), f32[768,256]{1,0:T(8,128)}) %reduce-scatter.2.cloned.1.call-update) | async-done | bytes 786448 | tf_op jit(solution)/shard_map/reduce_scatter | solution.py:37
  23.4 2.2 %broadcast_multiply_fusion = f32[768,256]{1,0:T(8,128)} fusion(f32[768,256]{1,0:T(8,128)} %reduce-scatter.2.cloned.1.call-done, f32[768]{0:T(1024)S(1)} %rsqrt_reduce_fusion), kind=kLoop, calls=%fused_computation.19 | loop fusion | flops 196608 | bytes 1575936 | tf_op jit(solution)/shard_map/mul | solution.py:39
  25.6 0.0 all-gather.3.cloned.1.call-update
  25.6 0.0 all-gather.5.cloned.1.call-start
  25.7 0.7 compare_select_fusion
  26.4 0.1 reshape.134
  26.5 0.8 fusion.13
  27.2 63.3 %all-gather.3.cloned.1.call-done = f32[3072,256]{1,0:T(8,128)} async-done(((f32[768,256]{1,0:T(8,128)}), f32[3072,256]{1,0:T(8,128)}) %all-gather.3.cloned.1.call-update) | async-done | bytes 3145744 | tf_op jit(solution)/shard_map/all_gather | solution.py:39
  90.5 8.6 %gather_fusion = f32[36,256,256]{2,1,0:T(8,128)} fusion(f32[12,256,256]{2,1,0:T(8,128)} %bitcast.40, s32[1024]{0:T(1024)S(1)} %pad_clamp_fusion), kind=kCustom, calls=%fused_computation.clone | custom fusion | bytes 18874512 | tf_op jit(solution)/shard_map/jit(_take)/gather | solution.py:17
  99.1 11.0 %fusion.2 = f32[3,256,256,1]{2,1,3,0:T(8,128)S(1)} fusion(f32[3,12,256,256]{3,2,1,0:T(8,128)} %bitcast.39, f32[1,3,12,256,256]{4,3,2,1,0:T(8,128)} %param.10, f32[3,12]{1,0:T(4,128)S(1)} %get-tuple-element.10, pred[3,12]{1,0:T(4,128)(4,1)S(1)} %get-tuple-element.11), kind=kOutput, calls=%fused_computation.5 | convolution fusion | flops 3628597248 | bytes 19660980 | tf_op jit(solution)/shard_map/tkab,tkbw->taw/dot_general | solution.py:18
  110.1 1.1 fusion.10
  111.1 0.0 all-gather.5.cloned.1.call-update
  111.1 62.3 %all-gather.5.cloned.1.call-done = f32[3072,256]{1,0:T(8,128)} async-done(((f32[768,256]{1,0:T(8,128)}), f32[3072,256]{1,0:T(8,128)}) %all-gather.5.cloned.1.call-update) | async-done | bytes 3145744 | tf_op jit(solution)/shard_map/all_gather | solution.py:39
  173.5 8.6 %gather_fusion.1 = f32[36,256,256]{2,1,0:T(8,128)} fusion(f32[12,256,256]{2,1,0:T(8,128)} %bitcast.41, s32[1024]{0:T(1024)S(1)} %pad_clamp_fusion), kind=kCustom, calls=%fused_computation.1.clone | custom fusion | bytes 18874512 | tf_op jit(solution)/shard_map/jit(_take)/gather | solution.py:17
  182.0 0.0 copy-start.1
  182.0 11.0 %fusion = f32[3,256,256,1]{2,1,3,0:T(8,128)S(1)} fusion(f32[3,12,256,256]{3,2,1,0:T(8,128)} %bitcast.38, f32[1,3,12,256,256]{4,3,2,1,0:T(8,128)} %param.10, f32[3,12]{1,0:T(4,128)S(1)} %get-tuple-element.10, pred[3,12]{1,0:T(4,128)(4,1)S(1)} %get-tuple-element.11), kind=kOutput, calls=%fused_computation.3 | convolution fusion | flops 3628597248 | bytes 19660980 | tf_op jit(solution)/shard_map/tkab,tkbw->taw/dot_general | solution.py:18
  193.0 0.0 copy-done.1
  193.0 0.2 multiply_add_fusion
  193.2 0.1 slice_bitcast_fusion.3
  193.3 0.1 pad_maximum_fusion
  193.3 14.7 %all_to_all.5 = f32[4,1,192,256]{3,2,1,0:T(8,128)S(1)} all-to-all(f32[4,1,192,256]{3,2,1,0:T(8,128)S(1)} %pad_maximum_fusion), channel_id=1, replica_groups=mesh['rel'=4,'node'=4,'feat'=2] {'rel'}, dimensions={0} | all-to-all | bytes 1572864 | tf_op jit(solution)/shard_map/all_to_all | solution.py:10
  208.1 0.9 copy.18
  (1 shorter events, 0.0 us)
Async XLA Ops:
  6.5 1.3 copy-start
  6.5 16.9 %reduce-scatter.2.cloned.1.call-start = ((), (), s32[]{:S(2)}) async-start(), calls=%async_computation.2 | async-start | bytes 2359296 | tf_op jit(solution)/shard_map/reduce_scatter | solution.py:37
  11.5 79.0 %all-gather.3.cloned.1.call-start = ((), (), s32[]{:S(2)}) async-start(), calls=%async_computation.3 | async-start | bytes 3932160 | tf_op jit(solution)/shard_map/all_gather | solution.py:39
  25.6 147.8 %all-gather.5.cloned.1.call-start = ((), (), s32[]{:S(2)}) async-start(), calls=%async_computation.4 | async-start | bytes 3932160 | tf_op jit(solution)/shard_map/all_gather | solution.py:39
  182.0 11.0 %copy-start.1 = (f32[1,256]{1,0:T(1,128)S(1)}, f32[1,256]{1,0:T(1,128)}, u32[]{:S(2)}) copy-start(f32[1,256]{1,0:T(1,128)} %param.15) | copy-start | bytes 3076
Sparse Core Ops, SparseCore 0:
  11.6 11.7 reduce-scatter.1
  25.7 64.7 all-gather.2
  111.3 62.1 all-gather.4
